TPU v7x, 32 devices: a whole 2x2x4 slice. The times are simulated.
32 devices in a mesh: row: 8 (over z, core), col: 4 (over y, x).
Axes of the slice: x: 2, y: 2, z: 4, core: 2. Of those that a mesh axis runs over, the one named last changes fastest.
Arguments:
- rhs: bfloat16 [3, 8, 64, 256], P(None, 'row'), may hold values from -6 to 6
- dinv: bfloat16 [3, 8, 256, 256], P(None, 'row'), as said below
- tiles: bfloat16 [2, 8, 8, 256, 256], P(None, 'row', 'col'), may hold values from -0.09375 to 0.09375
- pattern: int32 [2, 2, 8, 8], P(None, None, 'row', 'col'), may hold values from 0 to 7, as said below
Outputs:
- solution: float32 [3, 8, 64, 256], P(None, 'row')
Inputs may be any that keep to these rules, and one draw needn't show every extreme that they name: pattern[0, l, p, t] = p; pattern[1, l, p, t] = j has (j) modulo the size of col equal to t // 2; positions may repeat, and repeated tiles add. `dinv`: lower triangular with a positive diagonal.
All inputs are finite; a program needn't handle non-finite values.
Results may differ from a plain program's by a relative error of at most 0.0055.
Values may be sent and summed in bfloat16 or wider, within the bound.
No kernel may reach another device: no remote copies, remote signals or barrier semaphores. Data moves between devices by JAX's collectives and lax.ppermute only.
A program may use at most 64 MiB of HBM per device.

v0:
```python
import jax
import jax.numpy as jnp
from jax import lax
from jax.sharding import PartitionSpec as P


def broadcast(block, axis, holder):
    block = jnp.where(lax.axis_index(axis) == holder, block, jnp.zeros_like(block))
    return lax.psum(block, axis)


def collect(rounded, mine_col, col_count, repeat):
    whole_level = lax.all_gather(rounded, "row", axis=0, tiled=True)
    shaped = whole_level.reshape((repeat, col_count) + rounded.shape)
    picked = lax.dynamic_index_in_dim(shaped, mine_col, 1, keepdims=False)
    return picked.reshape((-1,) + rounded.shape[1:])


def per_device(rhs, dinv, tiles, pattern):
    blocks = rhs.shape[1]
    levels_all = rhs.shape[0]
    col_count = lax.axis_size("col")
    row_count = lax.axis_size("row")
    repeat = row_count // col_count
    mine_row = lax.axis_index("row")
    mine_col = lax.axis_index("col")
    targets = pattern[0, :, 0, :] % blocks
    raw_cols = pattern[1, :, 0, :]
    sources = raw_cols // blocks // col_count * blocks + raw_cols % blocks
    row_pick = (targets[:, None, :] == jnp.arange(blocks, dtype=jnp.int32)[None, :, None]).astype(
        jnp.float32
    )
    col_pick = (
        sources[:, None, :] == jnp.arange(repeat * blocks, dtype=jnp.int32)[None, :, None]
    ).astype(jnp.float32)
    fronts = [rhs]
    forward_all = [[] for front in fronts]
    rounded_all = [None for front in fronts]
    for level_now in range(levels_all):
        front_index = 0
        front_level = fronts[front_index][level_now]
        current = front_level.astype(jnp.float32)
        if level_now > 0:
            nearby = collect(rounded_all[front_index], mine_col, col_count, repeat)
            source = jnp.take(nearby, sources[level_now - 1], axis=0)
            product = jnp.einsum(
                "sjb,sab->sja", source, tiles[level_now - 1, 0], preferred_element_type=jnp.float32
            )
            partial_value = jnp.sum(
                row_pick[level_now - 1][:, :, None, None] * product[None], axis=1
            )
            total_sum = lax.psum(partial_value, "col")
            current = current - total_sum
        solved = jnp.einsum(
            "rjb,rab->rja",
            current.astype(jnp.bfloat16),
            dinv[level_now],
            preferred_element_type=jnp.float32,
        )
        forward_all[front_index].append(solved)
        rounded_all[front_index] = solved.astype(jnp.bfloat16)
    backward_all = [[None] * levels_all for front in fronts]
    following_all = [None for front in fronts]
    for level_now in range(levels_all - 1, -1, -1):
        front_index = 0
        remainder = forward_all[front_index][level_now]
        if level_now < levels_all - 1:
            source = jnp.take(following_all[front_index], targets[level_now], axis=0)
            product = jnp.einsum(
                "sja,sab->sjb", source, tiles[level_now, 0], preferred_element_type=jnp.float32
            )
            partial_value = jnp.sum(col_pick[level_now][:, :, None, None] * product[None], axis=1)
            column_total = lax.psum(partial_value, "row")
            shaped = column_total.reshape((repeat, blocks) + column_total.shape[1:])
            picked = lax.dynamic_index_in_dim(shaped, mine_row // col_count, 0, keepdims=False)
            arrived = broadcast(picked, "col", mine_row % col_count)
            remainder = remainder - arrived
        solved = jnp.einsum(
            "rjb,rba->rja",
            remainder.astype(jnp.bfloat16),
            dinv[level_now],
            preferred_element_type=jnp.float32,
        )
        backward_all[front_index][level_now] = solved
        following_all[front_index] = solved.astype(jnp.bfloat16)
    front_index = 0
    levels_stack = jnp.stack(backward_all[front_index])
    return levels_stack


def solution(mesh):
    in_specs = (
        P(None, "row", None, None),
        P(None, "row", None, None),
        P(None, "row", "col", None, None),
        P(None, None, "row", "col"),
    )
    out_specs = P(None, "row", None, None)
    return jax.shard_map(
        per_device, mesh=mesh, in_specs=in_specs, out_specs=out_specs, check_vma=False
    )
```

profile of v0, /device:TPU:0, one launch (start us, length us, event | category | flops | bytes accessed | tf_op | source)
XLA Modules:
  0.0 337.1 jit_solution(15482950410898514648)
XLA Ops:
  6.5 0.0 copy-start.1
  6.5 0.0 all-reduce.7.cloned.1.call-start
  6.5 1.1 fusion.57
  7.7 0.0 slice-start
  7.7 15.9 %all-gather = bf16[512,256]{1,0:T(8,128)(2,1)S(1)} all-gather(bf16[64,256]{1,0:T(8,128)(2,1)S(1)} %get-tuple-element.15), channel_id=2, replica_groups=mesh['row'=8,'col'=4] {'row'}, dimensions={0}, use_global_device_ids=true | all-gather | bytes 294912 | tf_op jit(solution)/shard_map/all_gather | solution.py:13
  23.6 0.0 copy-start
  23.6 0.0 slice-done
  23.7 0.6 gather_fusion
  24.3 0.0 copy-done.1
  24.3 0.0 copy-start.2
  24.3 0.8 convolution_bitcast_fusion.2
  25.1 0.0 all-reduce.7.cloned.1.call-update
  25.1 0.0 all-reduce.9.cloned.1.call-start
  25.2 43.0 %all-reduce.7.cloned.1.call-done = f32[1,64,256]{2,1,0:T(8,128)} async-done(((f32[1,64,256]{2,1,0:T(8,128)}), f32[1,64,256]{2,1,0:T(8,128)}) %all-reduce.7.cloned.1.call-update) | async-done | bytes 65552 | tf_op jit(solution)/shard_map/psum | solution.py:52
  68.2 0.0 copy-done
  68.2 0.0 copy-done.2
  68.2 1.0 fusion.58
  69.2 14.3 %all-gather.1 = bf16[512,256]{1,0:T(8,128)(2,1)S(1)} all-gather(bf16[64,256]{1,0:T(8,128)(2,1)S(1)} %get-tuple-element.17), channel_id=3, replica_groups=mesh['row'=8,'col'=4] {'row'}, dimensions={0}, use_global_device_ids=true | all-gather | bytes 294912 | tf_op jit(solution)/shard_map/all_gather | solution.py:13
  83.5 0.5 gather_fusion.1
  84.0 0.8 convolution_bitcast_fusion.1
  84.9 0.0 all-reduce.9.cloned.1.call-update
  84.9 0.0 all-reduce.11.cloned.1.call-start
  84.9 41.9 %all-reduce.9.cloned.1.call-done = f32[1,64,256]{2,1,0:T(8,128)} async-done(((f32[1,64,256]{2,1,0:T(8,128)}), f32[1,64,256]{2,1,0:T(8,128)}) %all-reduce.9.cloned.1.call-update) | async-done | bytes 65552 | tf_op jit(solution)/shard_map/psum | solution.py:52
  126.9 1.1 fusion.59
  128.0 0.2 fusion.1
  128.2 0.8 multiply_reduce_fusion.1
  128.9 0.0 all-reduce.11.cloned.1.call-update
  128.9 0.0 all-reduce.13.cloned.1.call-start
  129.0 55.1 %all-reduce.11.cloned.1.call-done = f32[2,64,256]{2,1,0:T(8,128)} async-done(((f32[2,64,256]{2,1,0:T(8,128)}), f32[2,64,256]{2,1,0:T(8,128)}) %all-reduce.11.cloned.1.call-update) | async-done | bytes 131088 | tf_op jit(solution)/shard_map/psum | solution.py:73
  184.1 1.5 dynamic-slice_select_fusion.1
  185.6 0.0 all-reduce.13.cloned.1.call-update
  185.6 0.0 all-reduce.15.cloned.1.call-start
  185.7 42.1 %all-reduce.13.cloned.1.call-done = f32[1,64,256]{2,1,0:T(8,128)} async-done(((f32[1,64,256]{2,1,0:T(8,128)}), f32[1,64,256]{2,1,0:T(8,128)}) %all-reduce.13.cloned.1.call-update) | async-done | bytes 65552 | tf_op jit(solution)/shard_map/psum | solution.py:9
  227.8 1.0 fusion.64
  228.8 0.2 fusion.4
  228.9 0.7 multiply_reduce_fusion
  229.7 0.0 all-reduce.15.cloned.1.call-update
  229.7 0.0 all-reduce.17.cloned.1.call-start
  229.8 55.1 %all-reduce.15.cloned.1.call-done = f32[2,64,256]{2,1,0:T(8,128)} async-done(((f32[2,64,256]{2,1,0:T(8,128)}), f32[2,64,256]{2,1,0:T(8,128)}) %all-reduce.15.cloned.1.call-update) | async-done | bytes 131088 | tf_op jit(solution)/shard_map/psum | solution.py:73
  284.9 1.5 dynamic-slice_select_fusion
  286.4 0.0 all-reduce.17.cloned.1.call-update
  286.4 42.2 %all-reduce.17.cloned.1.call-done = f32[1,64,256]{2,1,0:T(8,128)} async-done(((f32[1,64,256]{2,1,0:T(8,128)}), f32[1,64,256]{2,1,0:T(8,128)}) %all-reduce.17.cloned.1.call-update) | async-done | bytes 65552 | tf_op jit(solution)/shard_map/psum | solution.py:9
  328.5 1.0 convolution_bitcast_fusion
  329.5 0.7 pad_maximum_fusion
  (8 shorter events, 0.1 us)
Async XLA Ops:
  6.5 17.7 %copy-start.1 = (bf16[2,1,2,256,256]{4,3,2,1,0:T(8,128)(2,1)S(1)}, bf16[2,1,2,256,256]{4,3,2,1,0:T(8,128)(2,1)}, u32[]{:S(2)}) copy-start(bf16[2,1,2,256,256]{4,3,2,1,0:T(8,128)(2,1)} %param.10) | copy-start | bytes 1572868
  6.5 61.6 %all-reduce.7.cloned.1.call-start = ((), (), s32[]{:S(2)}) async-start(), calls=%async_computation | async-start | bytes 131072 | tf_op jit(solution)/shard_map/psum | solution.py:52
  7.7 16.0 %slice-start = ((s32[2,2,1,2]{3,2,1,0:T(1,128)}), s32[1,2,1,2]{3,2,1,0:T(1,128)S(1)}, s32[]{:S(2)}) async-start(s32[2,2,1,2]{3,2,1,0:T(1,128)} %param.11), calls=%async_computation.6 | async-start | bytes 2048 | tf_op jit(solution)/shard_map/slice | solution.py:28
  23.6 44.5 %copy-start = (bf16[3,1,256,256]{3,2,1,0:T(8,128)(2,1)S(1)}, bf16[3,1,256,256]{3,2,1,0:T(8,128)(2,1)}, u32[]{:S(2)}) copy-start(bf16[3,1,256,256]{3,2,1,0:T(8,128)(2,1)} %param.9) | copy-start | bytes 1179652
  24.3 43.9 %copy-start.2 = (bf16[3,1,64,256]{3,2,1,0:T(8,128)(2,1)S(1)}, bf16[3,1,64,256]{3,2,1,0:T(8,128)(2,1)}, u32[]{:S(2)}) copy-start(bf16[3,1,64,256]{3,2,1,0:T(8,128)(2,1)} %param.8) | copy-start | bytes 294916
  25.1 101.7 %all-reduce.9.cloned.1.call-start = ((), (), s32[]{:S(2)}) async-start(), calls=%async_computation.1 | async-start | bytes 131072 | tf_op jit(solution)/shard_map/psum | solution.py:52
  84.9 99.2 %all-reduce.11.cloned.1.call-start = ((), (), s32[]{:S(2)}) async-start(), calls=%async_computation.2 | async-start | bytes 262144 | tf_op jit(solution)/shard_map/psum | solution.py:73
  128.9 98.8 %all-reduce.13.cloned.1.call-start = ((), (), s32[]{:S(2)}) async-start(), calls=%async_computation.3 | async-start | bytes 131072 | tf_op jit(solution)/shard_map/psum | solution.py:9
  185.6 99.3 %all-reduce.15.cloned.1.call-start = ((), (), s32[]{:S(2)}) async-start(), calls=%async_computation.4 | async-start | bytes 262144 | tf_op jit(solution)/shard_map/psum | solution.py:73
  229.7 98.8 %all-reduce.17.cloned.1.call-start = ((), (), s32[]{:S(2)}) async-start(), calls=%async_computation.5 | async-start | bytes 131072 | tf_op jit(solution)/shard_map/psum | solution.py:9
Sparse Core Ops, SparseCore 0:
  25.3 42.8 all-reduce.6
  85.0 41.7 all-reduce.8
  129.2 54.9 all-reduce.10
  186.8 40.8 all-reduce.12
  229.9 54.9 all-reduce.14
  287.6 40.8 all-reduce.16
where the time goes:
time: 337 us
  waiting for transfers between devices  279 us (83%)
  blocking collectives  30.2 us (9%)
  between operations  13.6 us (4%)
  matrix products  7.25 us (2%)
  other arithmetic  5.19 us (2%)
    psum x2, waiting for transfers between devices, per_device(): column_total = lax.psum(partial_value, 'row')  110 us
    psum x2, waiting for transfers between devices, per_device(): total_sum = lax.psum(partial_value, 'col')  84.9 us
    psum x2, waiting for transfers between devices, broadcast(): return lax.psum(block, axis)  84.3 us
    all_gather x2, blocking collectives, collect(): whole_level = lax.all_gather(rounded, 'row', axis=0, tiled=True)  30.2 us
  transfers between devices with their start and end apart: 6, of which 6 were waited for; matrix products, arithmetic and copies ran while one was open for 0% of the time, Pallas kernels for 0%

commit v1 on v0

--- a/solution.py
+++ b/solution.py
@@ -2,6 +2,27 @@
 import jax.numpy as jnp
 from jax import lax
 from jax.sharding import PartitionSpec as P
+
+
+def ring_gather(array, axis, dim):
+    size, index, rows = (lax.axis_size(axis), lax.axis_index(axis), array.shape[dim])
+    ahead = [(i, (i + 1) % size) for i in range(size)]
+    left = [(i, (i - 1) % size) for i in range(size)]
+    out = jnp.zeros((*array.shape[:dim], size * rows, *array.shape[dim + 1 :]), array.dtype)
+    out = lax.dynamic_update_slice_in_dim(out, array, index * rows, axis=dim)
+    from_left = from_right = array
+    halfway = size // 2
+    for step in range(1, halfway + 1):
+        from_left = lax.ppermute(from_left, axis, ahead)
+        out = lax.dynamic_update_slice_in_dim(
+            out, from_left, (index - step) % size * rows, axis=dim
+        )
+        if step < size - halfway:
+            from_right = lax.ppermute(from_right, axis, left)
+            out = lax.dynamic_update_slice_in_dim(
+                out, from_right, (index + step) % size * rows, axis=dim
+            )
+    return out
 
 
 def broadcast(block, axis, holder):
@@ -10,7 +31,7 @@
 
 
 def collect(rounded, mine_col, col_count, repeat):
-    whole_level = lax.all_gather(rounded, "row", axis=0, tiled=True)
+    whole_level = ring_gather(rounded, "row", 0)
     shaped = whole_level.reshape((repeat, col_count) + rounded.shape)
     picked = lax.dynamic_index_in_dim(shaped, mine_col, 1, keepdims=False)
     return picked.reshape((-1,) + rounded.shape[1:])

time: 337 us -> 345 us (1.024)
  blocking collectives: 30.2 us -> 0 us
  starting transfers between devices: 0.21 us -> 22.7 us
  waiting for transfers between devices: 279 us -> 294 us
    all_gather x2 -> x0, blocking collectives: 30.2 us -> none  [collect(): whole_level = lax.all_gather(rounded, 'row', axis=0, tiled=True)]
    ppermute x0 -> x14, starting transfers between devices: none -> 22.5 us  [the longest x6 21.9 us: ring_gather(): from_right = lax.ppermute(from_right, axis, left)]
    ppermute x0 -> x14, waiting for transfers between devices: none -> 19.9 us  [the longest x8 19.8 us: ring_gather(): from_left = lax.ppermute(from_left, axis, ahead)]
    psum x2, waiting for transfers between devices: 84.9 us -> 79.8 us  [per_device(): total_sum = lax.psum(partial_value, 'col')]
  transfers between devices with their start and end apart: 6 -> 20, of which waited for: 6 -> 15; matrix products, arithmetic and copies ran while one was open for 0% -> 0% of each run, Pallas kernels for 0% -> 0%
where the time goes in v1:
time: 345 us
  waiting for transfers between devices  294 us (85%)
  starting transfers between devices  22.7 us (7%)
  between operations  13.8 us (4%)
  matrix products  7.19 us (2%)
  other arithmetic  5.21 us (2%)
    psum x2, waiting for transfers between devices, per_device(): column_total = lax.psum(partial_value, 'row')  110 us
    psum x2, waiting for transfers between devices, broadcast(): return lax.psum(block, axis)  84.3 us
    psum x2, waiting for transfers between devices, per_device(): total_sum = lax.psum(partial_value, 'col')  79.8 us
    ppermute x6, starting transfers between devices, ring_gather(): from_right = lax.ppermute(from_right, axis, left)  21.9 us
    ppermute x8, waiting for transfers between devices, ring_gather(): from_left = lax.ppermute(from_left, axis, ahead)  19.8 us
  transfers between devices with their start and end apart: 20, of which 15 were waited for; matrix products, arithmetic and copies ran while one was open for 0% of the time, Pallas kernels for 0%

profile of v1, /device:TPU:0, one launch (start us, length us, event | category | flops | bytes accessed | tf_op | source)
XLA Modules:
  0.0 344.5 jit_solution(10908073853880852998)
XLA Ops:
  6.5 1.1 fusion.18
  7.6 0.1 broadcast.180.clone
  7.7 0.5 collective-permute-start
  8.3 4.1 %collective-permute-start.1 = (bf16[1,64,256]{2,1,0:T(8,128)(2,1)S(1)}, bf16[1,64,256]{2,1,0:T(8,128)(2,1)S(1)}, u32[]{:S(2)}, u32[]{:S(2)}) collective-permute-start(bf16[1,64,256]{2,1,0:T(8,128)(2,1)S(1)} %get-tuple-element.14), channel_id=1, source_target_pairs={{0,28},{4,0},{8,4},{12,8},{16,12},{20,16},{24,20},{28,24},{1,29},{... | collective-permute-start | bytes 98312 | tf_op jit(solution)/shard_map/ppermute | solution.py:21
  12.5 1.4 collective-permute-done
  13.9 0.1 collective-permute-done.1
  13.9 3.5 %collective-permute-start.3 = (bf16[1,64,256]{2,1,0:T(8,128)(2,1)S(1)}, bf16[1,64,256]{2,1,0:T(8,128)(2,1)S(1)}, u32[]{:S(2)}, u32[]{:S(2)}) collective-permute-start(bf16[1,64,256]{2,1,0:T(8,128)(2,1)S(1)} %collective-permute-done.1), channel_id=1, source_target_pairs={{0,28},{4,0},{8,4},{12,8},{16,12},{20,16},{24,20},{28,24},{1,29},{... | collective-permute-start | bytes 98312 | tf_op jit(solution)/shard_map/ppermute | solution.py:21
  17.5 1.6 collective-permute-done.2
  19.1 3.5 %collective-permute-start.5 = (bf16[1,64,256]{2,1,0:T(8,128)(2,1)S(1)}, bf16[1,64,256]{2,1,0:T(8,128)(2,1)S(1)}, u32[]{:S(2)}, u32[]{:S(2)}) collective-permute-start(bf16[1,64,256]{2,1,0:T(8,128)(2,1)S(1)} %collective-permute-done.3), channel_id=1, source_target_pairs={{0,28},{4,0},{8,4},{12,8},{16,12},{20,16},{24,20},{28,24},{1,29},{... | collective-permute-start | bytes 98312 | tf_op jit(solution)/shard_map/ppermute | solution.py:21
  22.7 1.6 collective-permute-done.4
  24.3 5.1 %collective-permute-done.6 = bf16[1,64,256]{2,1,0:T(8,128)(2,1)S(1)} collective-permute-done((bf16[1,64,256]{2,1,0:T(8,128)(2,1)S(1)}, bf16[1,64,256]{2,1,0:T(8,128)(2,1)S(1)}, u32[]{:S(2)}, u32[]{:S(2)}) %collective-permute-start.6) | collective-permute-done | bytes 32800 | tf_op jit(solution)/shard_map/ppermute | solution.py:16
  29.4 0.6 gather_fusion
  30.0 0.8 convolution_bitcast_fusion.2
  30.8 0.0 all-reduce.9.cloned.1.call-start
  30.9 40.6 %all-reduce.7.cloned.1.call-done = f32[1,64,256]{2,1,0:T(8,128)} async-done(((f32[1,64,256]{2,1,0:T(8,128)}), f32[1,64,256]{2,1,0:T(8,128)}) %all-reduce.7.cloned.1.call-update) | async-done | bytes 65552 | tf_op jit(solution)/shard_map/psum | solution.py:73
  71.5 1.0 fusion.15
  72.5 0.1 broadcast.180
  72.6 0.1 collective-permute-start.7
  72.7 3.5 %collective-permute-start.8 = (bf16[1,64,256]{2,1,0:T(8,128)(2,1)S(1)}, bf16[1,64,256]{2,1,0:T(8,128)(2,1)S(1)}, u32[]{:S(2)}, u32[]{:S(2)}) collective-permute-start(bf16[1,64,256]{2,1,0:T(8,128)(2,1)S(1)} %get-tuple-element.10), channel_id=1, source_target_pairs={{0,28},{4,0},{8,4},{12,8},{16,12},{20,16},{24,20},{28,24},{1,29},{... | collective-permute-start | bytes 98312 | tf_op jit(solution)/shard_map/ppermute | solution.py:21
  76.2 1.7 collective-permute-done.7
  77.9 3.6 %collective-permute-start.10 = (bf16[1,64,256]{2,1,0:T(8,128)(2,1)S(1)}, bf16[1,64,256]{2,1,0:T(8,128)(2,1)S(1)}, u32[]{:S(2)}, u32[]{:S(2)}) collective-permute-start(bf16[1,64,256]{2,1,0:T(8,128)(2,1)S(1)} %collective-permute-done.8), channel_id=1, source_target_pairs={{0,28},{4,0},{8,4},{12,8},{16,12},{20,16},{24,20},{28,24},{1,29},{... | collective-permute-start | bytes 98312 | tf_op jit(solution)/shard_map/ppermute | solution.py:21
  81.5 1.9 collective-permute-done.9
  83.4 3.6 %collective-permute-start.12 = (bf16[1,64,256]{2,1,0:T(8,128)(2,1)S(1)}, bf16[1,64,256]{2,1,0:T(8,128)(2,1)S(1)}, u32[]{:S(2)}, u32[]{:S(2)}) collective-permute-start(bf16[1,64,256]{2,1,0:T(8,128)(2,1)S(1)} %collective-permute-done.10), channel_id=1, source_target_pairs={{0,28},{4,0},{8,4},{12,8},{16,12},{20,16},{24,20},{28,24},{1,29},{... | collective-permute-start | bytes 98312 | tf_op jit(solution)/shard_map/ppermute | solution.py:21
  87.0 1.5 collective-permute-done.11
  88.5 0.0 collective-permute-done.12
  88.6 5.1 %collective-permute-done.13 = bf16[1,64,256]{2,1,0:T(8,128)(2,1)S(1)} collective-permute-done((bf16[1,64,256]{2,1,0:T(8,128)(2,1)S(1)}, bf16[1,64,256]{2,1,0:T(8,128)(2,1)S(1)}, u32[]{:S(2)}, u32[]{:S(2)}) %collective-permute-start.13) | collective-permute-done | bytes 32800 | tf_op jit(solution)/shard_map/ppermute | solution.py:16
  93.7 0.6 gather_fusion.1
  94.2 0.8 convolution_bitcast_fusion.1
  95.1 0.0 all-reduce.9.cloned.1.call-update
  95.1 0.0 all-reduce.11.cloned.1.call-start
  95.2 39.2 %all-reduce.9.cloned.1.call-done = f32[1,64,256]{2,1,0:T(8,128)} async-done(((f32[1,64,256]{2,1,0:T(8,128)}), f32[1,64,256]{2,1,0:T(8,128)}) %all-reduce.9.cloned.1.call-update) | async-done | bytes 65552 | tf_op jit(solution)/shard_map/psum | solution.py:73
  134.3 1.1 fusion.57
  135.5 0.2 fusion.1
  135.6 0.8 multiply_reduce_fusion.1
  136.4 0.0 all-reduce.13.cloned.1.call-start
  136.5 55.1 %all-reduce.11.cloned.1.call-done = f32[2,64,256]{2,1,0:T(8,128)} async-done(((f32[2,64,256]{2,1,0:T(8,128)}), f32[2,64,256]{2,1,0:T(8,128)}) %all-reduce.11.cloned.1.call-update) | async-done | bytes 131088 | tf_op jit(solution)/shard_map/psum | solution.py:94
  191.6 1.5 dynamic-slice_select_fusion.1
  193.1 0.0 all-reduce.15.cloned.1.call-start
  193.1 42.1 %all-reduce.13.cloned.1.call-done = f32[1,64,256]{2,1,0:T(8,128)} async-done(((f32[1,64,256]{2,1,0:T(8,128)}), f32[1,64,256]{2,1,0:T(8,128)}) %all-reduce.13.cloned.1.call-update) | async-done | bytes 65552 | tf_op jit(solution)/shard_map/psum | solution.py:30
  235.2 1.0 fusion.62
  236.2 0.2 fusion.4
  236.4 0.7 multiply_reduce_fusion
  237.2 0.0 all-reduce.17.cloned.1.call-start
  237.2 55.1 %all-reduce.15.cloned.1.call-done = f32[2,64,256]{2,1,0:T(8,128)} async-done(((f32[2,64,256]{2,1,0:T(8,128)}), f32[2,64,256]{2,1,0:T(8,128)}) %all-reduce.15.cloned.1.call-update) | async-done | bytes 131088 | tf_op jit(solution)/shard_map/psum | solution.py:94
  292.3 1.5 dynamic-slice_select_fusion
  293.8 42.2 %all-reduce.17.cloned.1.call-done = f32[1,64,256]{2,1,0:T(8,128)} async-done(((f32[1,64,256]{2,1,0:T(8,128)}), f32[1,64,256]{2,1,0:T(8,128)}) %all-reduce.17.cloned.1.call-update) | async-done | bytes 65552 | tf_op jit(solution)/shard_map/psum | solution.py:30
  336.0 1.0 convolution_bitcast_fusion
  337.0 0.7 pad_maximum_fusion
  (48 shorter events, 0.3 us)
Async XLA Ops:
  6.5 65.0 %all-reduce.7.cloned.1.call-start = ((), (), s32[]{:S(2)}) async-start(), calls=%async_computation | async-start | bytes 131072 | tf_op jit(solution)/shard_map/psum | solution.py:73
  7.6 4.7 %slice-start = ((s32[2,2,1,2]{3,2,1,0:T(1,128)}), s32[1,2,1,2]{3,2,1,0:T(1,128)S(1)}, s32[]{:S(2)}) async-start(s32[2,2,1,2]{3,2,1,0:T(1,128)} %param.11), calls=%async_computation.6 | async-start | bytes 2048 | tf_op jit(solution)/shard_map/slice | solution.py:49
  7.7 22.3 %copy-start.1 = (bf16[2,1,2,256,256]{4,3,2,1,0:T(8,128)(2,1)S(1)}, bf16[2,1,2,256,256]{4,3,2,1,0:T(8,128)(2,1)}, u32[]{:S(2)}) copy-start(bf16[2,1,2,256,256]{4,3,2,1,0:T(8,128)(2,1)} %param.10) | copy-start | bytes 1572868
  7.7 6.2 %collective-permute-start = (bf16[1,64,256]{2,1,0:T(8,128)(2,1)S(1)}, bf16[1,64,256]{2,1,0:T(8,128)(2,1)S(1)}, u32[]{:S(2)}, u32[]{:S(2)}) collective-permute-start(bf16[1,64,256]{2,1,0:T(8,128)(2,1)S(1)} %get-tuple-element.14), channel_id=1, source_target_pairs={{0,4},{4,8},{8,12},{12,16},{16,20},{20,24},{24,28},{28,0},{1,5},{5... | collective-permute-start | bytes 98312 | tf_op jit(solution)/shard_map/ppermute | solution.py:16
  8.3 5.7 %collective-permute-start.1 = (bf16[1,64,256]{2,1,0:T(8,128)(2,1)S(1)}, bf16[1,64,256]{2,1,0:T(8,128)(2,1)S(1)}, u32[]{:S(2)}, u32[]{:S(2)}) collective-permute-start(bf16[1,64,256]{2,1,0:T(8,128)(2,1)S(1)} %get-tuple-element.14), channel_id=1, source_target_pairs={{0,28},{4,0},{8,4},{12,8},{16,12},{20,16},{24,20},{28,24},{1,29},{... | collective-permute-start | bytes 98312 | tf_op jit(solution)/shard_map/ppermute | solution.py:21
  13.9 5.2 %collective-permute-start.2 = (bf16[1,64,256]{2,1,0:T(8,128)(2,1)S(1)}, bf16[1,64,256]{2,1,0:T(8,128)(2,1)S(1)}, u32[]{:S(2)}, u32[]{:S(2)}) collective-permute-start(bf16[1,64,256]{2,1,0:T(8,128)(2,1)S(1)} %collective-permute-done), channel_id=1, source_target_pairs={{0,4},{4,8},{8,12},{12,16},{16,20},{20,24},{24,28},{28,0},{1,5},{5... | collective-permute-start | bytes 98312 | tf_op jit(solution)/shard_map/ppermute | solution.py:16
  13.9 5.2 %collective-permute-start.3 = (bf16[1,64,256]{2,1,0:T(8,128)(2,1)S(1)}, bf16[1,64,256]{2,1,0:T(8,128)(2,1)S(1)}, u32[]{:S(2)}, u32[]{:S(2)}) collective-permute-start(bf16[1,64,256]{2,1,0:T(8,128)(2,1)S(1)} %collective-permute-done.1), channel_id=1, source_target_pairs={{0,28},{4,0},{8,4},{12,8},{16,12},{20,16},{24,20},{28,24},{1,29},{... | collective-permute-start | bytes 98312 | tf_op jit(solution)/shard_map/ppermute | solution.py:21
  19.1 5.1 %collective-permute-start.4 = (bf16[1,64,256]{2,1,0:T(8,128)(2,1)S(1)}, bf16[1,64,256]{2,1,0:T(8,128)(2,1)S(1)}, u32[]{:S(2)}, u32[]{:S(2)}) collective-permute-start(bf16[1,64,256]{2,1,0:T(8,128)(2,1)S(1)} %collective-permute-done.2), channel_id=1, source_target_pairs={{0,4},{4,8},{8,12},{12,16},{16,20},{20,24},{24,28},{28,0},{1,5},{5... | collective-permute-start | bytes 98312 | tf_op jit(solution)/shard_map/ppermute | solution.py:16
  19.1 5.1 %collective-permute-start.5 = (bf16[1,64,256]{2,1,0:T(8,128)(2,1)S(1)}, bf16[1,64,256]{2,1,0:T(8,128)(2,1)S(1)}, u32[]{:S(2)}, u32[]{:S(2)}) collective-permute-start(bf16[1,64,256]{2,1,0:T(8,128)(2,1)S(1)} %collective-permute-done.3), channel_id=1, source_target_pairs={{0,28},{4,0},{8,4},{12,8},{16,12},{20,16},{24,20},{28,24},{1,29},{... | collective-permute-start | bytes 98312 | tf_op jit(solution)/shard_map/ppermute | solution.py:21
  24.3 5.1 %collective-permute-start.6 = (bf16[1,64,256]{2,1,0:T(8,128)(2,1)S(1)}, bf16[1,64,256]{2,1,0:T(8,128)(2,1)S(1)}, u32[]{:S(2)}, u32[]{:S(2)}) collective-permute-start(bf16[1,64,256]{2,1,0:T(8,128)(2,1)S(1)} %collective-permute-done.4), channel_id=1, source_target_pairs={{0,4},{4,8},{8,12},{12,16},{16,20},{20,24},{24,28},{28,0},{1,5},{5... | collective-permute-start | bytes 98312 | tf_op jit(solution)/shard_map/ppermute | solution.py:16
  24.3 47.2 %copy-start = (bf16[3,1,256,256]{3,2,1,0:T(8,128)(2,1)S(1)}, bf16[3,1,256,256]{3,2,1,0:T(8,128)(2,1)}, u32[]{:S(2)}) copy-start(bf16[3,1,256,256]{3,2,1,0:T(8,128)(2,1)} %param.9) | copy-start | bytes 1179652
  30.0 41.6 %copy-start.2 = (bf16[3,1,64,256]{3,2,1,0:T(8,128)(2,1)S(1)}, bf16[3,1,64,256]{3,2,1,0:T(8,128)(2,1)}, u32[]{:S(2)}) copy-start(bf16[3,1,64,256]{3,2,1,0:T(8,128)(2,1)} %param.8) | copy-start | bytes 294916
  30.8 103.5 %all-reduce.9.cloned.1.call-start = ((), (), s32[]{:S(2)}) async-start(), calls=%async_computation.1 | async-start | bytes 131072 | tf_op jit(solution)/shard_map/psum | solution.py:73
  72.6 5.3 %collective-permute-start.7 = (bf16[1,64,256]{2,1,0:T(8,128)(2,1)S(1)}, bf16[1,64,256]{2,1,0:T(8,128)(2,1)S(1)}, u32[]{:S(2)}, u32[]{:S(2)}) collective-permute-start(bf16[1,64,256]{2,1,0:T(8,128)(2,1)S(1)} %get-tuple-element.10), channel_id=1, source_target_pairs={{0,4},{4,8},{8,12},{12,16},{16,20},{20,24},{24,28},{28,0},{1,5},{5... | collective-permute-start | bytes 98312 | tf_op jit(solution)/shard_map/ppermute | solution.py:16
  72.7 5.2 %collective-permute-start.8 = (bf16[1,64,256]{2,1,0:T(8,128)(2,1)S(1)}, bf16[1,64,256]{2,1,0:T(8,128)(2,1)S(1)}, u32[]{:S(2)}, u32[]{:S(2)}) collective-permute-start(bf16[1,64,256]{2,1,0:T(8,128)(2,1)S(1)} %get-tuple-element.10), channel_id=1, source_target_pairs={{0,28},{4,0},{8,4},{12,8},{16,12},{20,16},{24,20},{28,24},{1,29},{... | collective-permute-start | bytes 98312 | tf_op jit(solution)/shard_map/ppermute | solution.py:21
  77.9 5.5 %collective-permute-start.9 = (bf16[1,64,256]{2,1,0:T(8,128)(2,1)S(1)}, bf16[1,64,256]{2,1,0:T(8,128)(2,1)S(1)}, u32[]{:S(2)}, u32[]{:S(2)}) collective-permute-start(bf16[1,64,256]{2,1,0:T(8,128)(2,1)S(1)} %collective-permute-done.7), channel_id=1, source_target_pairs={{0,4},{4,8},{8,12},{12,16},{16,20},{20,24},{24,28},{28,0},{1,5},{5... | collective-permute-start | bytes 98312 | tf_op jit(solution)/shard_map/ppermute | solution.py:16
  77.9 5.5 %collective-permute-start.10 = (bf16[1,64,256]{2,1,0:T(8,128)(2,1)S(1)}, bf16[1,64,256]{2,1,0:T(8,128)(2,1)S(1)}, u32[]{:S(2)}, u32[]{:S(2)}) collective-permute-start(bf16[1,64,256]{2,1,0:T(8,128)(2,1)S(1)} %collective-permute-done.8), channel_id=1, source_target_pairs={{0,28},{4,0},{8,4},{12,8},{16,12},{20,16},{24,20},{28,24},{1,29},{... | collective-permute-start | bytes 98312 | tf_op jit(solution)/shard_map/ppermute | solution.py:21
  83.4 5.1 %collective-permute-start.11 = (bf16[1,64,256]{2,1,0:T(8,128)(2,1)S(1)}, bf16[1,64,256]{2,1,0:T(8,128)(2,1)S(1)}, u32[]{:S(2)}, u32[]{:S(2)}) collective-permute-start(bf16[1,64,256]{2,1,0:T(8,128)(2,1)S(1)} %collective-permute-done.9), channel_id=1, source_target_pairs={{0,4},{4,8},{8,12},{12,16},{16,20},{20,24},{24,28},{28,0},{1,5},{5... | collective-permute-start | bytes 98312 | tf_op jit(solution)/shard_map/ppermute | solution.py:16
  83.4 5.2 %collective-permute-start.12 = (bf16[1,64,256]{2,1,0:T(8,128)(2,1)S(1)}, bf16[1,64,256]{2,1,0:T(8,128)(2,1)S(1)}, u32[]{:S(2)}, u32[]{:S(2)}) collective-permute-start(bf16[1,64,256]{2,1,0:T(8,128)(2,1)S(1)} %collective-permute-done.10), channel_id=1, source_target_pairs={{0,28},{4,0},{8,4},{12,8},{16,12},{20,16},{24,20},{28,24},{1,29},{... | collective-permute-start | bytes 98312 | tf_op jit(solution)/shard_map/ppermute | solution.py:21
  88.5 5.1 %collective-permute-start.13 = (bf16[1,64,256]{2,1,0:T(8,128)(2,1)S(1)}, bf16[1,64,256]{2,1,0:T(8,128)(2,1)S(1)}, u32[]{:S(2)}, u32[]{:S(2)}) collective-permute-start(bf16[1,64,256]{2,1,0:T(8,128)(2,1)S(1)} %collective-permute-done.11), channel_id=1, source_target_pairs={{0,4},{4,8},{8,12},{12,16},{16,20},{20,24},{24,28},{28,0},{1,5},{5... | collective-permute-start | bytes 98312 | tf_op jit(solution)/shard_map/ppermute | solution.py:16
  95.1 96.5 %all-reduce.11.cloned.1.call-start = ((), (), s32[]{:S(2)}) async-start(), calls=%async_computation.2 | async-start | bytes 262144 | tf_op jit(solution)/shard_map/psum | solution.py:94
  136.4 98.8 %all-reduce.13.cloned.1.call-start = ((), (), s32[]{:S(2)}) async-start(), calls=%async_computation.3 | async-start | bytes 131072 | tf_op jit(solution)/shard_map/psum | solution.py:30
  193.1 99.3 %all-reduce.15.cloned.1.call-start = ((), (), s32[]{:S(2)}) async-start(), calls=%async_computation.4 | async-start | bytes 262144 | tf_op jit(solution)/shard_map/psum | solution.py:94
  237.2 98.8 %all-reduce.17.cloned.1.call-start = ((), (), s32[]{:S(2)}) async-start(), calls=%async_computation.5 | async-start | bytes 131072 | tf_op jit(solution)/shard_map/psum | solution.py:30
Sparse Core Ops, SparseCore 0:
  31.0 40.5 all-reduce.6
  95.2 39.0 all-reduce.8
  136.6 54.9 all-reduce.10
  194.3 40.8 all-reduce.12
  237.4 54.9 all-reduce.14
  295.1 40.8 all-reduce.16
